TPU v7x, 32 devices: a whole 2x2x4 slice. The times are simulated.
32 devices in a mesh: parts: 2 (over y), row: 4 (over z), col: 4 (over x, core).
Axes of the slice: x: 2, y: 2, z: 4, core: 2. Of those that a mesh axis runs over, the one named last changes fastest.
Arguments:
- state: float32 [10, 128, 512], P(None, ('parts', 'row'), 'col'), parts along dimension 1, may hold values from -5 to 5
- history: float32 [10, 128, 512], P(None, ('parts', 'row'), 'col'), parts along dimension 1, may hold values from -5 to 5
- rates: float32 [10, 10, 128, 512], P(None, None, ('parts', 'row'), 'col'), parts along dimension 2, may hold values from -2 to 2
- quadratic: float32 [10, 128, 512], P(None, ('parts', 'row'), 'col'), parts along dimension 1, may hold values from 0.1 to 1
- velocity: float32 [10, 2], replicated, may hold values from -1.5 to 1.5
- precond: float32 [10, 10, 128, 512], P(None, None, ('parts', 'row'), 'col'), parts along dimension 2, may hold values from -1 to 2, as said below
Outputs:
- updated: float32 [10, 128, 512], P(None, ('parts', 'row'), 'col'), parts along dimension 1
- lin_residual: float32 [2], P('parts'), parts along dimension 0
There are 2 independent parts, one for each index of `parts`. A program takes and returns all parts, laid end to end along the dimension named above; an argument that names none is the same for every part. Nothing has to cross between parts.
Inputs may be any that keep to these rules, and one draw needn't show every extreme that they name: `precond`: each cell's block has diagonal entries 1 plus a spread term and independent off-diagonal entries.
All inputs are finite; a program needn't handle non-finite values.
Results may differ from a plain program's by a relative error of at most 0.00011.
Values sent between devices are 32-bit elements; how exact they have to be, the bound alone decides.
A program may use at most 64 MiB of HBM per device.

v0:
```python
import jax
import jax.numpy as jnp
from jax import lax
from jax.sharding import PartitionSpec as P

KRYLOV = 4


step_gamma = 0.4
tiny_eps = 1e-12


def extended(block, sides, width):
    for axis, dim in sides:
        count = lax.axis_size(axis)
        forward = [(i, i + 1) for i in range(count - 1)]
        backward = [(target, source) for source, target in forward]
        low = lax.ppermute(
            lax.slice_in_dim(block, block.shape[dim] - width, None, axis=dim), axis, forward
        )
        high = lax.ppermute(lax.slice_in_dim(block, 0, width, axis=dim), axis, backward)
        block = jnp.concatenate([low, block, high], axis=dim)
    return block


def advect(field, velocity):
    padded = extended(field, (("row", 1), ("col", 2)), 1)
    along_x = padded[:, 2:, 1:-1] - padded[:, :-2, 1:-1]
    along_y = padded[:, 1:-1, 2:] - padded[:, 1:-1, :-2]
    return -0.5 * (
        velocity[:, 0][:, None, None] * along_x + velocity[:, 1][:, None, None] * along_y
    )


def blockmul(matrix, field):
    return jnp.sum(matrix * field[None], axis=1)


def least_squares(hessen, beta):
    width = hessen.shape[1]
    rotated = jnp.zeros((width + 1,), jnp.float32).at[0].set(beta)
    upper = hessen
    for index in range(width):
        first = upper[index, index]
        second = upper[index + 1, index]
        radius = jnp.sqrt(first * first + second * second)
        cosine = first / radius
        sine = second / radius
        row_top = cosine * upper[index] + sine * upper[index + 1]
        row_low = -sine * upper[index] + cosine * upper[index + 1]
        upper = upper.at[index].set(row_top).at[index + 1].set(row_low)
        g_top = cosine * rotated[index] + sine * rotated[index + 1]
        g_low = -sine * rotated[index] + cosine * rotated[index + 1]
        rotated = rotated.at[index].set(g_top).at[index + 1].set(g_low)
    coef = jnp.zeros((width,), jnp.float32)
    for index in reversed(range(width)):
        partial_sum = jnp.sum(upper[index, index + 1 : width] * coef[index + 1 : width])
        coef = coef.at[index].set((rotated[index] - partial_sum) / upper[index, index])
    return (coef, jnp.abs(rotated[width]))


def body(state, history, rates, quadratic, velocity, precond):
    forcing = advect(state, velocity) + blockmul(rates, state) - quadratic * state * state
    rhs = -(state - history - step_gamma * forcing)
    beta = jnp.sqrt(lax.psum(jnp.sum(rhs * rhs), ("row", "col")) + tiny_eps)
    basis = [rhs / beta]
    kept = []
    hessen = jnp.zeros((KRYLOV + 1, KRYLOV), jnp.float32)
    for index in range(KRYLOV):
        direct = blockmul(precond, basis[index])
        kept.append(direct)
        jac = advect(direct, velocity) + blockmul(rates, direct) - 2.0 * quadratic * state * direct
        vector = direct - step_gamma * jac
        stacked = jnp.stack(basis)
        local_dots = jnp.sum(stacked * vector[None], axis=(1, 2, 3))
        dots, before = lax.psum((local_dots, jnp.sum(vector * vector)), ("row", "col"))
        vector = vector - jnp.sum(dots[:, None, None, None] * stacked, axis=0)
        squared = before - jnp.sum(dots * dots)
        size_new = jnp.sqrt(squared + tiny_eps)
        hessen = hessen.at[: index + 1, index].set(dots).at[index + 1, index].set(size_new)
        basis.append(vector / size_new)
    coef, lin_norm = least_squares(hessen, beta)
    combined = jnp.sum(coef[:, None, None, None] * jnp.stack(basis[:KRYLOV]), axis=0)
    correction = blockmul(precond, combined)
    return (state + correction, jnp.reshape(lin_norm, (1,)))


def solution(mesh):
    placed = (
        P(None, ("parts", "row"), "col"),
        P(None, ("parts", "row"), "col"),
        P(None, None, ("parts", "row"), "col"),
        P(None, ("parts", "row"), "col"),
        P(),
        P(None, None, ("parts", "row"), "col"),
    )
    return jax.shard_map(
        body,
        mesh=mesh,
        in_specs=placed,
        out_specs=(P(None, ("parts", "row"), "col"), P("parts")),
        check_vma=False,
    )
```

profile of v0, /device:TPU:0, one launch (start us, length us, event | category | flops | bytes accessed | tf_op | source)
XLA Modules:
  0.0 279.6 jit_solution(16215169505555502827)
XLA Ops:
  1.4 1.3 collective-permute-start
  2.7 5.6 %collective-permute-start.1 = (f32[10,1,128]{2,1,0:T(1,128)S(1)}, f32[10,1,128]{2,1,0:T(1,128)S(1)}, u32[]{:S(2)}, u32[]{:S(2)}) collective-permute-start(f32[10,1,128]{2,1,0:T(1,128)S(1)} %get-tuple-element.388), channel_id=1, source_target_pairs={{0,4},{4,8},{8,12},{1,5},{5,9},{9,13},{2,6},{6,10},{10,14},{3,7},{... | collective-permute-start | bytes 15368 | tf_op jit(solution)/shard_map/ppermute | solution.py:18
  8.4 1.3 multiply_reduce_fusion.9
  12.5 1.3 collective-permute-start.2
  13.8 3.0 %collective-permute-start.3 = (f32[10,18,1]{2,1,0:T(8,128)S(1)}, f32[10,18,1]{2,1,0:T(8,128)S(1)}, u32[]{:S(2)}, u32[]{:S(2)}) collective-permute-start(f32[10,18,1]{2,1,0:T(8,128)S(1)} %get-tuple-element.379), channel_id=1, source_target_pairs={{0,1},{1,2},{2,3},{4,5},{5,6},{6,7},{8,9},{9,10},{10,11},{12,13},{... | collective-permute-start | bytes 2168 | tf_op jit(solution)/shard_map/ppermute | solution.py:18
  18.6 33.0 %psum.63 = f32[]{:T(128)} all-reduce(f32[]{:T(128)} %get-tuple-element.368), channel_id=1, replica_groups=mesh['parts'=2,'row'=4,'col'=4] {'row','col'}, use_global_device_ids=true, to_apply=%region_2.0 | all-reduce | flops 1 | bytes 8 | tf_op jit(solution)/shard_map/psum | solution.py:65
  52.4 1.4 collective-permute-start.4
  53.9 4.5 %collective-permute-start.5 = (f32[10,1,128]{2,1,0:T(1,128)S(1)}, f32[10,1,128]{2,1,0:T(1,128)S(1)}, u32[]{:S(2)}, u32[]{:S(2)}) collective-permute-start(f32[10,1,128]{2,1,0:T(1,128)S(1)} %get-tuple-element.386), channel_id=1, source_target_pairs={{0,4},{4,8},{8,12},{1,5},{5,9},{9,13},{2,6},{6,10},{10,14},{3,7},{... | collective-permute-start | bytes 15368 | tf_op jit(solution)/shard_map/ppermute | solution.py:18
  59.9 1.3 collective-permute-start.6
  61.2 3.0 %collective-permute-start.7 = (f32[10,18,1]{2,1,0:T(8,128)S(1)}, f32[10,18,1]{2,1,0:T(8,128)S(1)}, u32[]{:S(2)}, u32[]{:S(2)}) collective-permute-start(f32[10,18,1]{2,1,0:T(8,128)S(1)} %get-tuple-element.377), channel_id=1, source_target_pairs={{0,1},{1,2},{2,3},{4,5},{5,6},{6,7},{8,9},{9,10},{10,11},{12,13},{... | collective-permute-start | bytes 2168 | tf_op jit(solution)/shard_map/ppermute | solution.py:18
  66.0 31.1 %all-reduce.6 = (f32[]{:T(128)}, f32[1]{0:T(128)}) all-reduce(f32[]{:T(128)} %get-tuple-element.351, f32[1]{0:T(128)} %bitcast.2), channel_id=1, replica_groups=mesh['parts'=2,'row'=4,'col'=4] {'row','col'}, use_global_device_ids=true, to_apply=%region_8.0 | all-reduce | flops 2 | bytes 16 | tf_op jit(solution)/shard_map/psum | solution.py:76
  99.8 1.3 collective-permute-start.8
  101.1 4.5 %collective-permute-start.9 = (f32[10,1,128]{2,1,0:T(1,128)S(1)}, f32[10,1,128]{2,1,0:T(1,128)S(1)}, u32[]{:S(2)}, u32[]{:S(2)}) collective-permute-start(f32[10,1,128]{2,1,0:T(1,128)S(1)} %get-tuple-element.384), channel_id=1, source_target_pairs={{0,4},{4,8},{8,12},{1,5},{5,9},{9,13},{2,6},{6,10},{10,14},{3,7},{... | collective-permute-start | bytes 15368 | tf_op jit(solution)/shard_map/ppermute | solution.py:18
  107.1 1.3 collective-permute-start.10
  108.4 3.0 %collective-permute-start.11 = (f32[10,18,1]{2,1,0:T(8,128)S(1)}, f32[10,18,1]{2,1,0:T(8,128)S(1)}, u32[]{:S(2)}, u32[]{:S(2)}) collective-permute-start(f32[10,18,1]{2,1,0:T(8,128)S(1)} %get-tuple-element.375), channel_id=1, source_target_pairs={{0,1},{1,2},{2,3},{4,5},{5,6},{6,7},{8,9},{9,10},{10,11},{12,13},{... | collective-permute-start | bytes 2168 | tf_op jit(solution)/shard_map/ppermute | solution.py:18
  113.3 31.0 %all-reduce.5 = (f32[2]{0:T(128)S(1)}, f32[]{:T(128)}) all-reduce(f32[2]{0:T(128)S(1)} %multiply_reduce_fusion.15, f32[]{:T(128)} %get-tuple-element.364), channel_id=1, replica_groups=mesh['parts'=2,'row'=4,'col'=4] {'row','col'}, use_global_device_ids=true, to_apply=%region_13.0 | all-reduce | flops 3 | bytes 24 | tf_op jit(solution)/shard_map/psum | solution.py:76
  146.6 1.3 collective-permute-start.12
  147.9 4.5 %collective-permute-start.13 = (f32[10,1,128]{2,1,0:T(1,128)S(1)}, f32[10,1,128]{2,1,0:T(1,128)S(1)}, u32[]{:S(2)}, u32[]{:S(2)}) collective-permute-start(f32[10,1,128]{2,1,0:T(1,128)S(1)} %get-tuple-element.382), channel_id=1, source_target_pairs={{0,4},{4,8},{8,12},{1,5},{5,9},{9,13},{2,6},{6,10},{10,14},{3,7},{... | collective-permute-start | bytes 15368 | tf_op jit(solution)/shard_map/ppermute | solution.py:18
  152.4 1.9 broadcast_select_fusion.2
  154.4 1.3 collective-permute-start.14
  155.8 3.0 %collective-permute-start.15 = (f32[10,18,1]{2,1,0:T(8,128)S(1)}, f32[10,18,1]{2,1,0:T(8,128)S(1)}, u32[]{:S(2)}, u32[]{:S(2)}) collective-permute-start(f32[10,18,1]{2,1,0:T(8,128)S(1)} %get-tuple-element.373), channel_id=1, source_target_pairs={{0,1},{1,2},{2,3},{4,5},{5,6},{6,7},{8,9},{9,10},{10,11},{12,13},{... | collective-permute-start | bytes 2168 | tf_op jit(solution)/shard_map/ppermute | solution.py:18
  158.9 1.4 scatter.60
  161.3 30.3 %all-reduce.4 = (f32[3]{0:T(128)S(1)}, f32[]{:T(128)}) all-reduce(f32[3]{0:T(128)S(1)} %multiply_reduce_fusion.13, f32[]{:T(128)} %get-tuple-element.362), channel_id=1, replica_groups=mesh['parts'=2,'row'=4,'col'=4] {'row','col'}, use_global_device_ids=true, to_apply=%region_22.0 | all-reduce | flops 4 | bytes 32 | tf_op jit(solution)/shard_map/psum | solution.py:76
  193.7 1.3 collective-permute-start.16
  195.0 4.5 %collective-permute-start.17 = (f32[10,1,128]{2,1,0:T(1,128)S(1)}, f32[10,1,128]{2,1,0:T(1,128)S(1)}, u32[]{:S(2)}, u32[]{:S(2)}) collective-permute-start(f32[10,1,128]{2,1,0:T(1,128)S(1)} %get-tuple-element.380), channel_id=1, source_target_pairs={{0,4},{4,8},{8,12},{1,5},{5,9},{9,13},{2,6},{6,10},{10,14},{3,7},{... | collective-permute-start | bytes 15368 | tf_op jit(solution)/shard_map/ppermute | solution.py:18
  199.6 1.9 broadcast_select_fusion.1
  201.6 1.3 collective-permute-start.18
  202.9 3.0 %collective-permute-start.19 = (f32[10,18,1]{2,1,0:T(8,128)S(1)}, f32[10,18,1]{2,1,0:T(8,128)S(1)}, u32[]{:S(2)}, u32[]{:S(2)}) collective-permute-start(f32[10,18,1]{2,1,0:T(8,128)S(1)} %get-tuple-element.371), channel_id=1, source_target_pairs={{0,1},{1,2},{2,3},{4,5},{5,6},{6,7},{8,9},{9,10},{10,11},{12,13},{... | collective-permute-start | bytes 2168 | tf_op jit(solution)/shard_map/ppermute | solution.py:18
  206.0 1.4 scatter.64
  208.5 30.7 %all-reduce.3 = (f32[4]{0:T(128)S(1)}, f32[]{:T(128)}) all-reduce(f32[4]{0:T(128)S(1)} %multiply_reduce_fusion.11, f32[]{:T(128)} %get-tuple-element.360), channel_id=1, replica_groups=mesh['parts'=2,'row'=4,'col'=4] {'row','col'}, use_global_device_ids=true, to_apply=%region_31.0 | all-reduce | flops 5 | bytes 40 | tf_op jit(solution)/shard_map/psum | solution.py:76
  241.1 2.0 broadcast_select_fusion
  243.1 1.3 scatter.66
  (123 shorter events, 26.5 us)
Async XLA Ops:
  1.4 10.9 %collective-permute-start = (f32[10,1,128]{2,1,0:T(1,128)S(1)}, f32[10,1,128]{2,1,0:T(1,128)S(1)}, u32[]{:S(2)}, u32[]{:S(2)}) collective-permute-start(f32[10,1,128]{2,1,0:T(1,128)S(1)} %get-tuple-element.389), channel_id=1, source_target_pairs={{4,0},{8,4},{12,8},{5,1},{9,5},{13,9},{6,2},{10,6},{14,10},{7,3},{... | collective-permute-start | bytes 15368 | tf_op jit(solution)/shard_map/ppermute | solution.py:21
  2.7 5.6 %copy-start.5 = (f32[10,2]{0,1:T(2,128)S(1)}, f32[10,2]{0,1:T(2,128)}, u32[]{:S(2)}) copy-start(f32[10,2]{0,1:T(2,128)} %param.68) | copy-start | bytes 244
  2.7 9.6 %collective-permute-start.1 = (f32[10,1,128]{2,1,0:T(1,128)S(1)}, f32[10,1,128]{2,1,0:T(1,128)S(1)}, u32[]{:S(2)}, u32[]{:S(2)}) collective-permute-start(f32[10,1,128]{2,1,0:T(1,128)S(1)} %get-tuple-element.388), channel_id=1, source_target_pairs={{0,4},{4,8},{8,12},{1,5},{5,9},{9,13},{2,6},{6,10},{10,14},{3,7},{... | collective-permute-start | bytes 15368 | tf_op jit(solution)/shard_map/ppermute | solution.py:18
  8.4 2.0 copy-start.6
  8.4 2.7 copy-start.7
  8.4 4.0 %copy-start.2 = (f32[10,16,128]{2,1,0:T(8,128)S(1)}, f32[10,16,128]{2,1,0:T(8,128)}, u32[]{:S(2)}) copy-start(f32[10,16,128]{2,1,0:T(8,128)} %param.64) | copy-start | bytes 245764
  8.4 9.4 %copy-start.3 = (f32[10,16,128]{2,1,0:T(8,128)S(1)}, f32[10,16,128]{2,1,0:T(8,128)}, u32[]{:S(2)}) copy-start(f32[10,16,128]{2,1,0:T(8,128)} %param.67) | copy-start | bytes 245764
  8.4 9.4 %copy-start.4 = (f32[10,16,128]{2,1,0:T(8,128)S(1)}, f32[10,16,128]{2,1,0:T(8,128)}, u32[]{:S(2)}) copy-start(f32[10,16,128]{2,1,0:T(8,128)} %param.65) | copy-start | bytes 245764
  9.7 42.6 %copy-start.1 = (f32[10,10,16,128]{3,2,1,0:T(8,128)S(1)}, f32[10,10,16,128]{3,2,1,0:T(8,128)}, u32[]{:S(2)}) copy-start(f32[10,10,16,128]{3,2,1,0:T(8,128)} %param.69) | copy-start | bytes 2457604
  12.5 4.4 %collective-permute-start.2 = (f32[10,18,1]{2,1,0:T(8,128)S(1)}, f32[10,18,1]{2,1,0:T(8,128)S(1)}, u32[]{:S(2)}, u32[]{:S(2)}) collective-permute-start(f32[10,18,1]{2,1,0:T(8,128)S(1)} %get-tuple-element.378), channel_id=1, source_target_pairs={{1,0},{2,1},{3,2},{5,4},{6,5},{7,6},{9,8},{10,9},{11,10},{13,12},{... | collective-permute-start | bytes 2168 | tf_op jit(solution)/shard_map/ppermute | solution.py:21
  13.8 4.0 %collective-permute-start.3 = (f32[10,18,1]{2,1,0:T(8,128)S(1)}, f32[10,18,1]{2,1,0:T(8,128)S(1)}, u32[]{:S(2)}, u32[]{:S(2)}) collective-permute-start(f32[10,18,1]{2,1,0:T(8,128)S(1)} %get-tuple-element.379), channel_id=1, source_target_pairs={{0,1},{1,2},{2,3},{4,5},{5,6},{6,7},{8,9},{9,10},{10,11},{12,13},{... | collective-permute-start | bytes 2168 | tf_op jit(solution)/shard_map/ppermute | solution.py:18
  52.3 11.9 %copy-start = (f32[10,10,16,128]{3,2,1,0:T(8,128)S(1)}, f32[10,10,16,128]{3,2,1,0:T(8,128)}, u32[]{:S(2)}) copy-start(f32[10,10,16,128]{3,2,1,0:T(8,128)} %param.66) | copy-start | bytes 2457604
  52.4 7.2 %collective-permute-start.4 = (f32[10,1,128]{2,1,0:T(1,128)S(1)}, f32[10,1,128]{2,1,0:T(1,128)S(1)}, u32[]{:S(2)}, u32[]{:S(2)}) collective-permute-start(f32[10,1,128]{2,1,0:T(1,128)S(1)} %get-tuple-element.387), channel_id=1, source_target_pairs={{4,0},{8,4},{12,8},{5,1},{9,5},{13,9},{6,2},{10,6},{14,10},{7,3},{... | collective-permute-start | bytes 15368 | tf_op jit(solution)/shard_map/ppermute | solution.py:21
  53.9 5.9 %collective-permute-start.5 = (f32[10,1,128]{2,1,0:T(1,128)S(1)}, f32[10,1,128]{2,1,0:T(1,128)S(1)}, u32[]{:S(2)}, u32[]{:S(2)}) collective-permute-start(f32[10,1,128]{2,1,0:T(1,128)S(1)} %get-tuple-element.386), channel_id=1, source_target_pairs={{0,4},{4,8},{8,12},{1,5},{5,9},{9,13},{2,6},{6,10},{10,14},{3,7},{... | collective-permute-start | bytes 15368 | tf_op jit(solution)/shard_map/ppermute | solution.py:18
  59.9 4.4 %collective-permute-start.6 = (f32[10,18,1]{2,1,0:T(8,128)S(1)}, f32[10,18,1]{2,1,0:T(8,128)S(1)}, u32[]{:S(2)}, u32[]{:S(2)}) collective-permute-start(f32[10,18,1]{2,1,0:T(8,128)S(1)} %get-tuple-element.376), channel_id=1, source_target_pairs={{1,0},{2,1},{3,2},{5,4},{6,5},{7,6},{9,8},{10,9},{11,10},{13,12},{... | collective-permute-start | bytes 2168 | tf_op jit(solution)/shard_map/ppermute | solution.py:21
  61.2 4.0 %collective-permute-start.7 = (f32[10,18,1]{2,1,0:T(8,128)S(1)}, f32[10,18,1]{2,1,0:T(8,128)S(1)}, u32[]{:S(2)}, u32[]{:S(2)}) collective-permute-start(f32[10,18,1]{2,1,0:T(8,128)S(1)} %get-tuple-element.377), channel_id=1, source_target_pairs={{0,1},{1,2},{2,3},{4,5},{5,6},{6,7},{8,9},{9,10},{10,11},{12,13},{... | collective-permute-start | bytes 2168 | tf_op jit(solution)/shard_map/ppermute | solution.py:18
  99.8 5.9 %collective-permute-start.8 = (f32[10,1,128]{2,1,0:T(1,128)S(1)}, f32[10,1,128]{2,1,0:T(1,128)S(1)}, u32[]{:S(2)}, u32[]{:S(2)}) collective-permute-start(f32[10,1,128]{2,1,0:T(1,128)S(1)} %get-tuple-element.385), channel_id=1, source_target_pairs={{4,0},{8,4},{12,8},{5,1},{9,5},{13,9},{6,2},{10,6},{14,10},{7,3},{... | collective-permute-start | bytes 15368 | tf_op jit(solution)/shard_map/ppermute | solution.py:21
  101.1 5.9 %collective-permute-start.9 = (f32[10,1,128]{2,1,0:T(1,128)S(1)}, f32[10,1,128]{2,1,0:T(1,128)S(1)}, u32[]{:S(2)}, u32[]{:S(2)}) collective-permute-start(f32[10,1,128]{2,1,0:T(1,128)S(1)} %get-tuple-element.384), channel_id=1, source_target_pairs={{0,4},{4,8},{8,12},{1,5},{5,9},{9,13},{2,6},{6,10},{10,14},{3,7},{... | collective-permute-start | bytes 15368 | tf_op jit(solution)/shard_map/ppermute | solution.py:18
  107.1 5.2 %collective-permute-start.10 = (f32[10,18,1]{2,1,0:T(8,128)S(1)}, f32[10,18,1]{2,1,0:T(8,128)S(1)}, u32[]{:S(2)}, u32[]{:S(2)}) collective-permute-start(f32[10,18,1]{2,1,0:T(8,128)S(1)} %get-tuple-element.374), channel_id=1, source_target_pairs={{1,0},{2,1},{3,2},{5,4},{6,5},{7,6},{9,8},{10,9},{11,10},{13,12},{... | collective-permute-start | bytes 2168 | tf_op jit(solution)/shard_map/ppermute | solution.py:21
  108.4 4.0 %collective-permute-start.11 = (f32[10,18,1]{2,1,0:T(8,128)S(1)}, f32[10,18,1]{2,1,0:T(8,128)S(1)}, u32[]{:S(2)}, u32[]{:S(2)}) collective-permute-start(f32[10,18,1]{2,1,0:T(8,128)S(1)} %get-tuple-element.375), channel_id=1, source_target_pairs={{0,1},{1,2},{2,3},{4,5},{5,6},{6,7},{8,9},{9,10},{10,11},{12,13},{... | collective-permute-start | bytes 2168 | tf_op jit(solution)/shard_map/ppermute | solution.py:18
  146.6 7.7 %collective-permute-start.12 = (f32[10,1,128]{2,1,0:T(1,128)S(1)}, f32[10,1,128]{2,1,0:T(1,128)S(1)}, u32[]{:S(2)}, u32[]{:S(2)}) collective-permute-start(f32[10,1,128]{2,1,0:T(1,128)S(1)} %get-tuple-element.383), channel_id=1, source_target_pairs={{4,0},{8,4},{12,8},{5,1},{9,5},{13,9},{6,2},{10,6},{14,10},{7,3},{... | collective-permute-start | bytes 15368 | tf_op jit(solution)/shard_map/ppermute | solution.py:21
  147.9 6.4 %collective-permute-start.13 = (f32[10,1,128]{2,1,0:T(1,128)S(1)}, f32[10,1,128]{2,1,0:T(1,128)S(1)}, u32[]{:S(2)}, u32[]{:S(2)}) collective-permute-start(f32[10,1,128]{2,1,0:T(1,128)S(1)} %get-tuple-element.382), channel_id=1, source_target_pairs={{0,4},{4,8},{8,12},{1,5},{5,9},{9,13},{2,6},{6,10},{10,14},{3,7},{... | collective-permute-start | bytes 15368 | tf_op jit(solution)/shard_map/ppermute | solution.py:18
  154.4 6.0 %collective-permute-start.14 = (f32[10,18,1]{2,1,0:T(8,128)S(1)}, f32[10,18,1]{2,1,0:T(8,128)S(1)}, u32[]{:S(2)}, u32[]{:S(2)}) collective-permute-start(f32[10,18,1]{2,1,0:T(8,128)S(1)} %get-tuple-element.372), channel_id=1, source_target_pairs={{1,0},{2,1},{3,2},{5,4},{6,5},{7,6},{9,8},{10,9},{11,10},{13,12},{... | collective-permute-start | bytes 2168 | tf_op jit(solution)/shard_map/ppermute | solution.py:21
  155.8 4.7 %collective-permute-start.15 = (f32[10,18,1]{2,1,0:T(8,128)S(1)}, f32[10,18,1]{2,1,0:T(8,128)S(1)}, u32[]{:S(2)}, u32[]{:S(2)}) collective-permute-start(f32[10,18,1]{2,1,0:T(8,128)S(1)} %get-tuple-element.373), channel_id=1, source_target_pairs={{0,1},{1,2},{2,3},{4,5},{5,6},{6,7},{8,9},{9,10},{10,11},{12,13},{... | collective-permute-start | bytes 2168 | tf_op jit(solution)/shard_map/ppermute | solution.py:18
  193.7 7.8 %collective-permute-start.16 = (f32[10,1,128]{2,1,0:T(1,128)S(1)}, f32[10,1,128]{2,1,0:T(1,128)S(1)}, u32[]{:S(2)}, u32[]{:S(2)}) collective-permute-start(f32[10,1,128]{2,1,0:T(1,128)S(1)} %get-tuple-element.381), channel_id=1, source_target_pairs={{4,0},{8,4},{12,8},{5,1},{9,5},{13,9},{6,2},{10,6},{14,10},{7,3},{... | collective-permute-start | bytes 15368 | tf_op jit(solution)/shard_map/ppermute | solution.py:21
  195.0 6.5 %collective-permute-start.17 = (f32[10,1,128]{2,1,0:T(1,128)S(1)}, f32[10,1,128]{2,1,0:T(1,128)S(1)}, u32[]{:S(2)}, u32[]{:S(2)}) collective-permute-start(f32[10,1,128]{2,1,0:T(1,128)S(1)} %get-tuple-element.380), channel_id=1, source_target_pairs={{0,4},{4,8},{8,12},{1,5},{5,9},{9,13},{2,6},{6,10},{10,14},{3,7},{... | collective-permute-start | bytes 15368 | tf_op jit(solution)/shard_map/ppermute | solution.py:18
  201.6 5.9 %collective-permute-start.18 = (f32[10,18,1]{2,1,0:T(8,128)S(1)}, f32[10,18,1]{2,1,0:T(8,128)S(1)}, u32[]{:S(2)}, u32[]{:S(2)}) collective-permute-start(f32[10,18,1]{2,1,0:T(8,128)S(1)} %get-tuple-element.370), channel_id=1, source_target_pairs={{1,0},{2,1},{3,2},{5,4},{6,5},{7,6},{9,8},{10,9},{11,10},{13,12},{... | collective-permute-start | bytes 2168 | tf_op jit(solution)/shard_map/ppermute | solution.py:21
  202.9 4.6 %collective-permute-start.19 = (f32[10,18,1]{2,1,0:T(8,128)S(1)}, f32[10,18,1]{2,1,0:T(8,128)S(1)}, u32[]{:S(2)}, u32[]{:S(2)}) collective-permute-start(f32[10,18,1]{2,1,0:T(8,128)S(1)} %get-tuple-element.371), channel_id=1, source_target_pairs={{0,1},{1,2},{2,3},{4,5},{5,6},{6,7},{8,9},{9,10},{10,11},{12,13},{... | collective-permute-start | bytes 2168 | tf_op jit(solution)/shard_map/ppermute | solution.py:18
where the time goes:
time: 281 us; the launch traced here: 280 us
  blocking collectives  156 us (56%)
  starting transfers between devices  52 us (19%)
  between operations  33.8 us (12%)
  other arithmetic  19.4 us (7%)
  local copies, waits for them, and re-layouts  15 us (5%)
  waiting for transfers between devices  3.3 us (1%)
    psum x4, blocking collectives, body(): lax.psum((local_dots, jnp.sum(vector * vector)), ('row', 'col'))  123 us
    ppermute x10, starting transfers between devices, extended(): lax.ppermute(lax.slice_in_dim(block, block.shape[dim] - width, None, axis...  39 us
    psum x1, blocking collectives, body(): beta = jnp.sqrt(lax.psum(jnp.sum(rhs * rhs), ('row', 'col')) + tiny_eps)  33 us
    ppermute x10, starting transfers between devices, extended(): lax.ppermute(lax.slice_in_dim(block, 0, width, axis=dim), axis, backward)  13 us
    another operation x8, other arithmetic  7.82 us
  transfers between devices with their start and end apart: 20, of which 5 were waited for; matrix products, arithmetic and copies ran while one was open for 5% of the time, Pallas kernels for 0%

commit v1 on v0

v1 whole, which is shorter than its diff:
```python
import functools

import jax
import jax.numpy as jnp
from jax import lax
from jax.experimental import pallas as pl
from jax.experimental.pallas import tpu as pltpu
from jax.sharding import PartitionSpec as P

KRYLOV = 4
GAMMA = 0.4
EPS = 1e-12
SHIFT = 1.5
MESH = pl.DeviceIdType.MESH


def small_solve(gram):
    width = KRYLOV
    norm2 = gram[0][0] + EPS
    beta = jnp.sqrt(norm2)
    scale = 1.0 / norm2
    g = {(i, j): gram[j][i] * scale for j in range(width + 1) for i in range(j + 1)}
    one = jnp.ones_like(beta)
    tri = {(0, 0): one}
    inv = [one]
    sub = []
    for j in range(width + 1):
        for i in range(min(j, width)):
            value = g[i, j]
            for m in range(i):
                value = value - tri[m, i] * tri[m, j]
            tri[i, j] = value * inv[i]
        if j:
            left = g[j, j]
            for m in range(j):
                left = left - tri[m, j] * tri[m, j]
            size = jnp.sqrt(jnp.maximum(left, 0.0) * inv[j - 1] * inv[j - 1] + EPS)
            sub.append(size)
            tri[j, j] = tri[j - 1, j - 1] * size
            inv.append(1.0 / tri[j, j])
    hess = {}
    for k in range(width):
        for i in range(k + 1):
            value = tri[i, k + 1] + SHIFT * tri[i, k]
            for m in range(max(i - 1, 0), k):
                value = value - hess[i, m] * tri[m, k]
            hess[i, k] = value * inv[k]
        hess[k + 1, k] = sub[k]
    rot = [beta]
    for k in range(width):
        first, second = hess[k, k], hess[k + 1, k]
        inverse = 1.0 / jnp.sqrt(first * first + second * second)
        cosine, sine = first * inverse, second * inverse
        for j in range(k, width):
            top = hess[k, j]
            low = hess.get((k + 1, j))
            hess[k, j] = cosine * top + sine * low
            hess[k + 1, j] = cosine * low - sine * top
        rot.append(-sine * rot[k])
        rot[k] = cosine * rot[k]
    coef = [None] * width
    for k in reversed(range(width)):
        value = rot[k]
        for m in range(k + 1, width):
            value = value - hess[k, m] * coef[m]
        coef[k] = value / hess[k, k]
    out = [None] * width
    for k in reversed(range(width)):
        value = coef[k]
        for m in range(k + 1, width):
            value = value - tri[k, m] * out[m]
        out[k] = value * inv[k]
    return [c / beta for c in out], jnp.abs(rot[width])


def kernel(rows, cols, state_h, hist_h, rates_h, quad_h, vel, prec_h, out, lin,
           y, hist, rates, quad, prec, loads, vs, ds, diag, cx, cy, cs,
           put_lo, put_hi, put_t, got_lo, got_hi, got_l, got_r, ssem, rsem,
           grow, slots, gsend, grecv):
    species, high, wide = y.shape
    my_row, my_col = lax.axis_index("row"), lax.axis_index("col")
    count = rows * cols
    me = my_row * cols + my_col
    pairs = [(state_h, y), (rates_h, rates), (quad_h, quad), (hist_h, hist), (prec_h, prec)]
    copies = [pltpu.make_async_copy(a, b, loads.at[i]) for i, (a, b) in enumerate(pairs)]
    for copy in copies:
        copy.start()

    barrier = pltpu.get_barrier_semaphore()

    def other(o):
        index = lax.rem(me + o, count)
        return index, {"row": index // cols, "col": lax.rem(index, cols)}

    def greet(o, carry):
        pl.semaphore_signal(barrier, inc=1, device_id=other(o)[1], device_id_type=MESH)
        return carry

    lax.fori_loop(1, count, greet, 0)

    up, down = my_row > 0, my_row < rows - 1
    left, right = my_col > 0, my_col < cols - 1
    row_at = lax.broadcasted_iota(jnp.int32, (high, wide), 0)
    lane = lax.broadcasted_iota(jnp.int32, (high, wide), 1)
    pair = jnp.where(lane == wide - 1, 0, (lane + 1) // 2)
    edge = jnp.where(lane == 0, -1.0, jnp.where(lane == wide - 1, 1.0, 0.0))

    for there, ref in ((up, got_lo), (down, got_hi), (left, got_l), (right, got_r)):
        @pl.when(jnp.logical_not(there))
        def _(ref=ref):
            ref[...] = jnp.zeros_like(ref)

    for s in range(species):
        cx[s] = jnp.full((high, wide), 0.5 * GAMMA * vel[s, 0])
        cy[s] = jnp.full((high, wide), 0.5 * GAMMA * vel[s, 1])
        cs[s] = cy[s] * edge
    for k in range(1, KRYLOV):
        vs[k] = jnp.zeros_like(y)
    grow[...] = jnp.zeros_like(grow)

    def transfers(p):
        def make(src, dst, axis, mine, step, size, q):
            return pltpu.make_async_remote_copy(
                src_ref=src.at[p], dst_ref=dst.at[p], send_sem=ssem.at[p, q], recv_sem=rsem.at[p, q],
                device_id={axis: lax.rem(mine + step + size, size)}, device_id_type=MESH)
        return [
            (up, down, make(put_lo, got_hi, "row", my_row, -1, rows, 0)),
            (down, up, make(put_hi, got_lo, "row", my_row, 1, rows, 1)),
            (left, right, make(put_t, got_r, "col", my_col, -1, cols, 2)),
            (right, left, make(put_t, got_l, "col", my_col, 1, cols, 3)),
        ]

    def pack(p, v):
        put_lo[p] = v[:, 0:1, :]
        put_hi[p] = v[:, high - 1:high, :]
        tile = jnp.zeros((high, wide), jnp.float32)
        for s in range(species):
            moved = pltpu.roll(v[s], 2 * s, 1) if s else v[s]
            tile = jnp.where(pair == s, moved, tile)
        put_t[p] = tile

    def send(p):
        for sends, _, copy in transfers(p):
            @pl.when(sends)
            def _(copy=copy):
                copy.start()

    def receive(p):
        for _, gets, copy in transfers(p):
            @pl.when(gets)
            def _(copy=copy):
                copy.wait_recv()

    def sent(p):
        for sends, _, copy in transfers(p):
            @pl.when(sends)
            def _(copy=copy):
                copy.wait_send()

    def inner(v):
        parts = []
        for s in range(species):
            f = v[s]
            dx = jnp.where(row_at == high - 1, 0.0, pltpu.roll(f, high - 1, 0)) - jnp.where(
                row_at == 0, 0.0, pltpu.roll(f, 1, 0))
            dy = jnp.where(lane == wide - 1, 0.0, pltpu.roll(f, wide - 1, 1)) - jnp.where(
                lane == 0, 0.0, pltpu.roll(f, 1, 1))
            parts.append(cx[s] * dx + cy[s] * dy)
        return jnp.stack(parts)

    def outer(p):
        both = jnp.where(lax.rem(lane, 2) == 1, pltpu.roll(got_l[p], 2, 1), got_r[p])
        parts = []
        for s in range(species):
            moved = pltpu.roll(both, wide - 2 * s - 1, 1)
            ends = jnp.where(row_at == high - 1, got_hi[p, s], 0.0) - jnp.where(
                row_at == 0, got_lo[p, s], 0.0)
            parts.append(cx[s] * ends + cs[s] * moved)
        return jnp.stack(parts)

    def blockmul(matrix, field):
        total = matrix[:, 0] * field(0)[None]
        for t in range(1, species):
            total = total + matrix[:, t] * field(t)[None]
        return total

    def dots(k, upto):
        line = grow[...]
        at = lax.broadcasted_iota(jnp.int32, line.shape, 1)
        mine = vs[k]
        for j in range(upto):
            by_cell = jnp.sum(mine * vs[j], axis=0)
            value = jnp.sum(jnp.sum(by_cell, axis=0, keepdims=True), axis=1, keepdims=True)
            line = jnp.where(at == k * (KRYLOV + 1) + j, value, line)
        grow[...] = line

    copies[0].wait()
    pack(0, y[...])
    pl.semaphore_wait(barrier, count - 1)
    send(0)
    copies[1].wait()
    copies[2].wait()
    copies[3].wait()
    now = y[...]
    loss = quad[...] * now
    diag[...] = 1.0 + (2.0 * GAMMA) * loss
    start = hist[...] - now - GAMMA * (loss * now) + GAMMA * blockmul(rates, lambda t: y[t]) - inner(now)
    copies[4].wait()
    receive(0)
    vs[0] = start - outer(0)

    def step(k, carry):
        ds[k] = blockmul(prec, lambda t: vs[k, t])
        d = ds[k]
        pack(k + 1, d)
        send(k + 1)
        w = diag[...] * d - SHIFT * vs[k] - GAMMA * blockmul(rates, lambda t: ds[k, t]) + inner(d)
        vs[k + 1] = w
        dots(k, KRYLOV)
        receive(k + 1)
        vs[k + 1] = vs[k + 1] + outer(k + 1)
        return carry

    lax.fori_loop(0, KRYLOV, step, 0)
    dots(KRYLOV, KRYLOV + 1)
    slots[me] = grow[...]

    def share(o):
        index, where = other(o)
        put = pltpu.make_async_remote_copy(
            src_ref=grow, dst_ref=slots.at[me], send_sem=gsend.at[o], recv_sem=grecv.at[me],
            device_id=where, device_id_type=MESH)
        take = pltpu.make_async_remote_copy(
            src_ref=grow, dst_ref=slots.at[index], send_sem=gsend.at[o], recv_sem=grecv.at[index],
            device_id=where, device_id_type=MESH)
        return put, take

    def put_all(o, carry):
        share(o)[0].start()
        return carry

    def take_all(o, carry):
        share(o)[1].wait_recv()
        return carry

    def put_done(o, carry):
        share(o)[0].wait_send()
        return carry

    lax.fori_loop(1, count, put_all, 0)
    for p in range(KRYLOV + 1):
        sent(p)
    lax.fori_loop(1, count, take_all, 0)
    total = jnp.sum(slots[...], axis=0)
    at = lax.broadcasted_iota(jnp.int32, total.shape, 1)
    gram = [[jnp.sum(jnp.where(at == k * (KRYLOV + 1) + j, total, 0.0), axis=1, keepdims=True)
             for j in range(k + 1)] for k in range(KRYLOV + 1)]
    coef, residual = small_solve(gram)
    lin[0] = residual[0, 0]
    result = y[...]
    for k in range(KRYLOV):
        result = result + jnp.broadcast_to(coef[k], (high, wide))[None] * ds[k]
    out[...] = result
    lax.fori_loop(1, count, put_done, 0)


def body(rows, cols, state, history, rates, quadratic, velocity, precond):
    species, high, wide = state.shape
    field = (species, high, wide)
    phases = KRYLOV + 1
    vmem = lambda *shape: pltpu.VMEM(shape, jnp.float32)
    anywhere = pl.BlockSpec(memory_space=pl.ANY)
    updated, residual = pl.pallas_call(
        functools.partial(kernel, rows, cols),
        out_shape=(jax.ShapeDtypeStruct(field, jnp.float32), jax.ShapeDtypeStruct((1,), jnp.float32)),
        in_specs=[anywhere] * 4 + [pl.BlockSpec(memory_space=pltpu.SMEM), anywhere],
        out_specs=(pl.BlockSpec(memory_space=pltpu.VMEM), pl.BlockSpec(memory_space=pltpu.SMEM)),
        scratch_shapes=[
            vmem(*field), vmem(*field), vmem(species, *field), vmem(*field), vmem(species, *field),
            pltpu.SemaphoreType.DMA((5,)),
            vmem(phases, *field), vmem(KRYLOV, *field),
            vmem(*field), vmem(*field), vmem(*field), vmem(*field),
            vmem(phases, species, 1, wide), vmem(phases, species, 1, wide), vmem(phases, high, wide),
            vmem(phases, species, 1, wide), vmem(phases, species, 1, wide),
            vmem(phases, high, wide), vmem(phases, high, wide),
            pltpu.SemaphoreType.DMA((phases, 4)), pltpu.SemaphoreType.DMA((phases, 4)),
            vmem(1, wide), vmem(rows * cols, 1, wide),
            pltpu.SemaphoreType.DMA((rows * cols,)), pltpu.SemaphoreType.DMA((rows * cols,)),
        ],
        compiler_params=pltpu.CompilerParams(collective_id=0, has_side_effects=True),
    )(state, history, rates, quadratic, velocity, precond)
    return updated, residual


def solution(mesh):
    cells = P(None, ("parts", "row"), "col")
    blocks = P(None, None, ("parts", "row"), "col")
    return jax.shard_map(
        functools.partial(body, mesh.shape["row"], mesh.shape["col"]),
        mesh=mesh,
        in_specs=(cells, cells, blocks, cells, P(), blocks),
        out_specs=(cells, P("parts")),
        check_vma=False,
    )
```

time: 281 us -> 32 us (0.11)
  blocking collectives: 156 us -> 0 us
  starting transfers between devices: 52 us -> 0 us
  between operations: 33.8 us -> 2.33 us
  Pallas kernels: 0 us -> 26.5 us
  other arithmetic: 19.4 us -> 0 us
  local copies, waits for them, and re-layouts: 15 us -> 2.89 us
  waiting for transfers between devices: 3.3 us -> 0 us
    psum x5 -> x0, blocking collectives: 156 us -> none  [the longest x4 123 us: body(): lax.psum((local_dots, jnp.sum(vector * vector)), ('row', 'col'))]
    ppermute x20 -> x0, starting transfers between devices: 52 us -> none  [the longest x10 39 us: extended(): lax.ppermute(lax.slice_in_dim(block, block.shape[dim] - width, None, axis...]
    pallas_call x0 -> x1, Pallas kernels: none -> 26.5 us  [body(): pl.pallas_call(functools.partial(kernel, rows, cols), out_shape=(jax.Shap...]
    reduce_sum x26 -> x0, other arithmetic: 9.8 us -> none  [the longest x3 2.36 us: body(): jnp.sum(vector * vector)]
    another operation x9 -> x0, other arithmetic: 7.83 us -> none
    slice x23 -> x0, local copies, waits for them, and re-layouts: 7.73 us -> none  [the longest x4 2.2 us: least_squares(): first = upper[index, index]]
    scatter x17 -> x0, local copies, waits for them, and re-layouts: 5.45 us -> none  [the longest x8 5.25 us: body(): hessen.at[:index + 1, index].set(dots).at[index + 1, index].set(size_new)]
    ppermute x20 -> x0, waiting for transfers between devices: 3.3 us -> none  [the longest x10 3.27 us: extended(): lax.ppermute(lax.slice_in_dim(block, block.shape[dim] - width, None, axis...]
  transfers between devices with their start and end apart: 20 -> 0, of which waited for: 5 -> 0; matrix products, arithmetic and copies ran while one was open for 5% -> 0% of each run, Pallas kernels for 0% -> 0%
where the time goes in v1:
time: 32 us; the launch traced here: 31.7 us
  Pallas kernels  26.5 us (83%)
  local copies, waits for them, and re-layouts  2.89 us (9%)
  between operations  2.33 us (7%)
    pallas_call x1, Pallas kernels, body(): pl.pallas_call(functools.partial(kernel, rows, cols), out_shape=(jax.Shap...  26.5 us
    unnamed x2, local copies, waits for them, and re-layouts  2.89 us

profile of v1, /device:TPU:0, one launch (start us, length us, event | category | flops | bytes accessed | tf_op | source)
XLA Modules:
  0.0 31.7 jit_solution(7835921052647232187)
XLA Ops:
  0.6 1.4 %copy.8.vel = f32[10,2]{1,0:T(8,128)} copy(f32[10,2]{0,1:T(2,128)} %param.10) | data formatting | bytes 160 | tf_op args[4]
  2.0 26.5 %shard_map.77 = (f32[10,16,128]{2,1,0:T(8,128)}, f32[1]{0:T(128)}) custom-call(f32[10,16,128]{2,1,0:T(8,128)} %state_h.1, f32[10,16,128]{2,1,0:T(8,128)} %hist_h.1, f32[10,10,16,128]{3,2,1,0:T(8,128)} %rates_h.1, f32[10,16,128]{2,1,0:T(8,128)} %quad_h.1, f32[10,2]{1,0:T(8,128)} %copy.8.vel, f32[10,10,16,128]{3,2,1,0:T(8,128)} %prec_h.1), custom_call_target="tpu_custom_call" | custom-call | tf_op jit(solution)/shard_map/pallas_call | solution.py:273
  28.5 1.5 %copy.11 = f32[10,16,128]{2,1,0:T(8,128)} copy(f32[10,16,128]{2,1,0:T(8,128)} %get-tuple-element.4) | data formatting | bytes 163840

commit v2 on v1

--- a/solution.py
+++ b/solution.py
@@ -73,15 +73,15 @@
     return [c / beta for c in out], jnp.abs(rot[width])
 
 
-def kernel(rows, cols, state_h, hist_h, rates_h, quad_h, vel, prec_h, out, lin,
-           y, hist, rates, quad, prec, loads, vs, ds, diag, cx, cy, cs,
+def kernel(rows, cols, state_h, hist_h, rates_h, quad_h, vel_h, prec_h, out, lin,
+           vel, y, hist, rates, quad, prec, loads, vs, ds, diag, cx, cy, cs,
            put_lo, put_hi, put_t, got_lo, got_hi, got_l, got_r, ssem, rsem,
            grow, slots, gsend, grecv):
     species, high, wide = y.shape
     my_row, my_col = lax.axis_index("row"), lax.axis_index("col")
     count = rows * cols
     me = my_row * cols + my_col
-    pairs = [(state_h, y), (rates_h, rates), (quad_h, quad), (hist_h, hist), (prec_h, prec)]
+    pairs = [(state_h, y), (vel_h, vel), (rates_h, rates), (quad_h, quad), (hist_h, hist), (prec_h, prec)]
     copies = [pltpu.make_async_copy(a, b, loads.at[i]) for i, (a, b) in enumerate(pairs)]
     for copy in copies:
         copy.start()
@@ -96,10 +96,18 @@
         pl.semaphore_signal(barrier, inc=1, device_id=other(o)[1], device_id_type=MESH)
         return carry
 
-    lax.fori_loop(1, count, greet, 0)
-
+
+    near = rows + cols - 2 <= KRYLOV + 2
     up, down = my_row > 0, my_row < rows - 1
     left, right = my_col > 0, my_col < cols - 1
+    if near:
+        for there, axis, at in ((up, "row", my_row - 1), (down, "row", my_row + 1), (left, "col", my_col - 1), (right, "col", my_col + 1)):
+            @pl.when(there)
+            def _(axis=axis, at=at):
+                pl.semaphore_signal(barrier, inc=1, device_id={axis: at}, device_id_type=MESH)
+    else:
+        lax.fori_loop(1, count, greet, 0)
+
     row_at = lax.broadcasted_iota(jnp.int32, (high, wide), 0)
     lane = lax.broadcasted_iota(jnp.int32, (high, wide), 1)
     pair = jnp.where(lane == wide - 1, 0, (lane + 1) // 2)
@@ -109,14 +117,6 @@
         @pl.when(jnp.logical_not(there))
         def _(ref=ref):
             ref[...] = jnp.zeros_like(ref)
-
-    for s in range(species):
-        cx[s] = jnp.full((high, wide), 0.5 * GAMMA * vel[s, 0])
-        cy[s] = jnp.full((high, wide), 0.5 * GAMMA * vel[s, 1])
-        cs[s] = cy[s] * edge
-    for k in range(1, KRYLOV):
-        vs[k] = jnp.zeros_like(y)
-    grow[...] = jnp.zeros_like(grow)
 
     def transfers(p):
         def make(src, dst, axis, mine, step, size, q):
@@ -131,8 +131,9 @@
         ]
 
     def pack(p, v):
-        put_lo[p] = v[:, 0:1, :]
-        put_hi[p] = v[:, high - 1:high, :]
+        for s in range(species):
+            put_lo[p, s:s + 1, :] = v[s, 0:1, :]
+            put_hi[p, s:s + 1, :] = v[s, high - 1:high, :]
         tile = jnp.zeros((high, wide), jnp.float32)
         for s in range(species):
             moved = pltpu.roll(v[s], 2 * s, 1) if s else v[s]
@@ -173,8 +174,8 @@
         parts = []
         for s in range(species):
             moved = pltpu.roll(both, wide - 2 * s - 1, 1)
-            ends = jnp.where(row_at == high - 1, got_hi[p, s], 0.0) - jnp.where(
-                row_at == 0, got_lo[p, s], 0.0)
+            ends = jnp.where(row_at == high - 1, got_hi[p, s:s + 1, :], 0.0) - jnp.where(
+                row_at == 0, got_lo[p, s:s + 1, :], 0.0)
             parts.append(cx[s] * ends + cs[s] * moved)
         return jnp.stack(parts)
 
@@ -196,16 +197,27 @@
 
     copies[0].wait()
     pack(0, y[...])
-    pl.semaphore_wait(barrier, count - 1)
+    if near:
+        beside = sum(there.astype(jnp.int32) for there in (up, down, left, right))
+        pl.semaphore_wait(barrier, beside)
+    else:
+        pl.semaphore_wait(barrier, count - 1)
     send(0)
     copies[1].wait()
-    copies[2].wait()
-    copies[3].wait()
+    for s in range(species):
+        cx[s] = jnp.full((high, wide), 0.5 * GAMMA * vel[0, s])
+        cy[s] = jnp.full((high, wide), 0.5 * GAMMA * vel[1, s])
+        cs[s] = cy[s] * edge
+    for k in range(1, KRYLOV):
+        vs[k] = jnp.zeros_like(y)
+    grow[...] = jnp.zeros_like(grow)
+    for copy in copies[2:5]:
+        copy.wait()
     now = y[...]
     loss = quad[...] * now
     diag[...] = 1.0 + (2.0 * GAMMA) * loss
     start = hist[...] - now - GAMMA * (loss * now) + GAMMA * blockmul(rates, lambda t: y[t]) - inner(now)
-    copies[4].wait()
+    copies[5].wait()
     receive(0)
     vs[0] = start - outer(0)
 
@@ -272,23 +284,24 @@
     anywhere = pl.BlockSpec(memory_space=pl.ANY)
     updated, residual = pl.pallas_call(
         functools.partial(kernel, rows, cols),
-        out_shape=(jax.ShapeDtypeStruct(field, jnp.float32), jax.ShapeDtypeStruct((1,), jnp.float32)),
-        in_specs=[anywhere] * 4 + [pl.BlockSpec(memory_space=pltpu.SMEM), anywhere],
+        out_shape=(pltpu.VMEM(field, jnp.float32), jax.ShapeDtypeStruct((1,), jnp.float32)),
+        in_specs=[anywhere] * 6,
         out_specs=(pl.BlockSpec(memory_space=pltpu.VMEM), pl.BlockSpec(memory_space=pltpu.SMEM)),
         scratch_shapes=[
+            pltpu.SMEM(velocity.shape[::-1], jnp.float32),
             vmem(*field), vmem(*field), vmem(species, *field), vmem(*field), vmem(species, *field),
-            pltpu.SemaphoreType.DMA((5,)),
+            pltpu.SemaphoreType.DMA((6,)),
             vmem(phases, *field), vmem(KRYLOV, *field),
             vmem(*field), vmem(*field), vmem(*field), vmem(*field),
-            vmem(phases, species, 1, wide), vmem(phases, species, 1, wide), vmem(phases, high, wide),
-            vmem(phases, species, 1, wide), vmem(phases, species, 1, wide),
+            vmem(phases, species, wide), vmem(phases, species, wide), vmem(phases, high, wide),
+            vmem(phases, species, wide), vmem(phases, species, wide),
             vmem(phases, high, wide), vmem(phases, high, wide),
             pltpu.SemaphoreType.DMA((phases, 4)), pltpu.SemaphoreType.DMA((phases, 4)),
             vmem(1, wide), vmem(rows * cols, 1, wide),
             pltpu.SemaphoreType.DMA((rows * cols,)), pltpu.SemaphoreType.DMA((rows * cols,)),
         ],
         compiler_params=pltpu.CompilerParams(collective_id=0, has_side_effects=True),
-    )(state, history, rates, quadratic, velocity, precond)
+    )(state, history, rates, quadratic, velocity.T, precond)
     return updated, residual
 
 

time: 32 us -> 27.8 us (0.87)
  local copies, waits for them, and re-layouts: 2.89 us -> 0.64 us
  Pallas kernels: 26.5 us -> 24.7 us
    unnamed x2 -> x1, local copies, waits for them, and re-layouts: 2.89 us -> 0.64 us
    pallas_call x1, Pallas kernels: 26.5 us -> 24.7 us  [body(): pl.pallas_call(functools.partial(kernel, rows, cols), out_shape=(pltpu.VM...]
where the time goes in v2:
time: 27.8 us; the launch traced here: 27.6 us
  Pallas kernels  24.7 us (89%)
  between operations  2.33 us (8%)
  local copies, waits for them, and re-layouts  0.64 us (2%)
    pallas_call x1, Pallas kernels, body(): pl.pallas_call(functools.partial(kernel, rows, cols), out_shape=(pltpu.VM...  24.7 us
    unnamed x1, local copies, waits for them, and re-layouts  0.64 us

profile of v2, /device:TPU:0, one launch (start us, length us, event | category | flops | bytes accessed | tf_op | source)
XLA Modules:
  0.0 27.6 jit_solution(10124151915638422674)
XLA Ops:
  0.6 24.7 %shard_map.77 = (f32[10,16,128]{2,1,0:T(8,128)S(1)}, f32[1]{0:T(128)}) custom-call(f32[10,16,128]{2,1,0:T(8,128)} %state_h.1, f32[10,16,128]{2,1,0:T(8,128)} %hist_h.1, f32[10,10,16,128]{3,2,1,0:T(8,128)} %rates_h.1, f32[10,16,128]{2,1,0:T(8,128)} %quad_h.1, f32[2,10]{1,0:T(2,128)} %bitcast.1, f32[10,10,16,128]{3,2,1,0:T(8,128)} %prec_h.1), custom_call_target="tpu_custom_call" | custom-call | tf_op jit(solution)/shard_map/pallas_call | solution.py:285
  25.3 0.6 %copy.10 = f32[10,16,128]{2,1,0:T(8,128)} copy(f32[10,16,128]{2,1,0:T(8,128)S(1)} %get-tuple-element.2) | data formatting | bytes 163840

commit v3 on v2

--- a/solution.py
+++ b/solution.py
@@ -76,7 +76,8 @@
 def kernel(rows, cols, state_h, hist_h, rates_h, quad_h, vel_h, prec_h, out, lin,
            vel, y, hist, rates, quad, prec, loads, vs, ds, diag, cx, cy, cs,
            put_lo, put_hi, put_t, got_lo, got_hi, got_l, got_r, ssem, rsem,
-           grow, slots, gsend, grecv):
+           grow, slots, gsend, grecv,
+           pput_lo, pput_hi, pput_t, pgot_lo, pgot_hi, pgot_l, pgot_r, psend, precv, got_c, csend, crecv):
     species, high, wide = y.shape
     my_row, my_col = lax.axis_index("row"), lax.axis_index("col")
     count = rows * cols
@@ -97,7 +98,7 @@
         return carry
 
 
-    near = rows + cols - 2 <= KRYLOV + 2
+    near = rows <= 4 and cols <= 4
     up, down = my_row > 0, my_row < rows - 1
     left, right = my_col > 0, my_col < cols - 1
     if near:
@@ -113,10 +114,45 @@
     pair = jnp.where(lane == wide - 1, 0, (lane + 1) // 2)
     edge = jnp.where(lane == 0, -1.0, jnp.where(lane == wide - 1, 1.0, 0.0))
 
-    for there, ref in ((up, got_lo), (down, got_hi), (left, got_l), (right, got_r)):
+    for there, ref in ((up, got_lo), (down, got_hi), (left, got_l), (right, got_r), (up, pgot_lo), (down, pgot_hi),
+                       (left, pgot_l), (right, pgot_r)):
         @pl.when(jnp.logical_not(there))
         def _(ref=ref):
             ref[...] = jnp.zeros_like(ref)
+
+    corners = []
+    for q, (dr, dc) in enumerate(((1, 1), (1, -1), (-1, 1), (-1, -1))):
+        sends = jnp.logical_and(down if dr > 0 else up, right if dc > 0 else left)
+        gets = jnp.logical_and(up if dr > 0 else down, left if dc > 0 else right)
+        corners.append((q, dr, dc, sends, gets))
+
+        @pl.when(jnp.logical_not(gets))
+        def _(q=q):
+            for p in range(1, KRYLOV, 2):
+                got_c[p, q] = jnp.zeros((1, wide), jnp.float32)
+
+    def diagonals(p):
+        made = []
+        for q, dr, dc, sends, gets in corners:
+            at = high - 1 if dr > 0 else 0
+            made.append((sends, gets, pltpu.make_async_remote_copy(
+                src_ref=put_t.at[p, at:at + 1], dst_ref=got_c.at[p, q],
+                send_sem=csend.at[p, q], recv_sem=crecv.at[p, q],
+                device_id={"row": lax.rem(my_row + dr + rows, rows), "col": lax.rem(my_col + dc + cols, cols)},
+                device_id_type=MESH)))
+        return made
+
+    def blocks():
+        def make(src, dst, axis, mine, step, size, q):
+            return pltpu.make_async_remote_copy(
+                src_ref=src, dst_ref=dst, send_sem=psend.at[q], recv_sem=precv.at[q],
+                device_id={axis: lax.rem(mine + step + size, size)}, device_id_type=MESH)
+        return [
+            (up, down, make(pput_lo, pgot_hi, "row", my_row, -1, rows, 0)),
+            (down, up, make(pput_hi, pgot_lo, "row", my_row, 1, rows, 1)),
+            (left, right, make(pput_t, pgot_r, "col", my_col, -1, cols, 2)),
+            (right, left, make(pput_t, pgot_l, "col", my_col, 1, cols, 3)),
+        ]
 
     def transfers(p):
         def make(src, dst, axis, mine, step, size, q):
@@ -130,33 +166,69 @@
             (right, left, make(put_t, got_l, "col", my_col, 1, cols, 3)),
         ]
 
+    def tile_of(v):
+        tile = jnp.zeros((high, wide), jnp.float32)
+        for s in range(species):
+            moved = pltpu.roll(v[s], 2 * s, 1) if s else v[s]
+            tile = jnp.where(pair == s, moved, tile)
+        return tile
+
     def pack(p, v):
         for s in range(species):
             put_lo[p, s:s + 1, :] = v[s, 0:1, :]
             put_hi[p, s:s + 1, :] = v[s, high - 1:high, :]
-        tile = jnp.zeros((high, wide), jnp.float32)
-        for s in range(species):
-            moved = pltpu.roll(v[s], 2 * s, 1) if s else v[s]
-            tile = jnp.where(pair == s, moved, tile)
-        put_t[p] = tile
-
-    def send(p):
-        for sends, _, copy in transfers(p):
+        put_t[p] = tile_of(v)
+
+    def pack_blocks():
+        def one(t, carry):
+            block = prec[:, t]
+            for s in range(species):
+                pput_lo[t, s:s + 1, :] = block[s, 0:1, :]
+                pput_hi[t, s:s + 1, :] = block[s, high - 1:high, :]
+            pput_t[t] = tile_of(block)
+            return carry
+        lax.fori_loop(0, species, one, 0)
+
+    def send(made):
+        for sends, _, copy in made:
             @pl.when(sends)
             def _(copy=copy):
                 copy.start()
 
-    def receive(p):
-        for _, gets, copy in transfers(p):
+    def receive(made):
+        for _, gets, copy in made:
             @pl.when(gets)
             def _(copy=copy):
                 copy.wait_recv()
 
-    def sent(p):
-        for sends, _, copy in transfers(p):
+    def sent(made):
+        for sends, _, copy in made:
             @pl.when(sends)
             def _(copy=copy):
                 copy.wait_send()
+
+    def complete(k, p):
+        low, top = got_lo[p + 1], got_hi[p + 1]
+        west, east = got_l[p + 1], got_r[p + 1]
+        first = lax.broadcasted_iota(jnp.int32, (1, wide), 1) == 0
+        near_row, far_row = row_at == 0, row_at == high - 1
+        lines = [got_c[p, q] for q in range(4)]
+        for t in range(species):
+            d = ds[k, t]
+            odd, even = (2 * t - 1) % wide, 2 * t
+            ul, dl = lines[0][:, odd:odd + 1], lines[2][:, odd:odd + 1]
+            ur, dr = lines[1][:, even:even + 1], lines[3][:, even:even + 1]
+            ax, ay, ends = cx[t], cy[t], cs[t, 0:1, :]
+            low = low + pgot_lo[t] * (ax[0:1] * d[0:1] + ends * jnp.where(first, ul, ur))
+            top = top + pgot_hi[t] * (ends * jnp.where(first, dl, dr) - ax[0:1] * d[high - 1:high])
+            side_l = jnp.where(near_row, -ul, jnp.where(far_row, dl, 0.0))
+            side_r = jnp.where(near_row, -ur, jnp.where(far_row, dr, 0.0))
+            west = west + pgot_l[t] * (ax * side_l + ay * d[:, 0:1])
+            east = east + pgot_r[t] * (ax * side_r - ay * d[:, wide - 1:wide])
+        got_lo[p + 1] = low
+        got_hi[p + 1] = top
+        got_l[p + 1] = west
+        got_r[p + 1] = east
 
     def inner(v):
         parts = []
@@ -202,7 +274,7 @@
         pl.semaphore_wait(barrier, beside)
     else:
         pl.semaphore_wait(barrier, count - 1)
-    send(0)
+    send(transfers(0))
     copies[1].wait()
     for s in range(species):
         cx[s] = jnp.full((high, wide), 0.5 * GAMMA * vel[0, s])
@@ -214,26 +286,45 @@
     for copy in copies[2:5]:
         copy.wait()
     now = y[...]
+    copies[5].wait()
+    pack_blocks()
+    send(blocks())
     loss = quad[...] * now
     diag[...] = 1.0 + (2.0 * GAMMA) * loss
     start = hist[...] - now - GAMMA * (loss * now) + GAMMA * blockmul(rates, lambda t: y[t]) - inner(now)
-    copies[5].wait()
-    receive(0)
+    receive(transfers(0))
     vs[0] = start - outer(0)
 
-    def step(k, carry):
+    def apply(k):
+        return diag[...] * ds[k] - SHIFT * vs[k] - GAMMA * blockmul(rates, lambda t: ds[k, t]) + inner(ds[k])
+
+    def two_steps(j, carry):
+        k, p = 2 * j, 2 * j + 1
         ds[k] = blockmul(prec, lambda t: vs[k, t])
-        d = ds[k]
-        pack(k + 1, d)
-        send(k + 1)
-        w = diag[...] * d - SHIFT * vs[k] - GAMMA * blockmul(rates, lambda t: ds[k, t]) + inner(d)
-        vs[k + 1] = w
+        pack(p, ds[k])
+        send(transfers(p))
+        send(diagonals(p))
+        vs[k + 1] = apply(k)
+        pack(p + 1, blockmul(prec, lambda t: vs[k + 1, t]))
+        send(transfers(p + 1))
         dots(k, KRYLOV)
-        receive(k + 1)
-        vs[k + 1] = vs[k + 1] + outer(k + 1)
+
+        @pl.when(j == 0)
+        def _():
+            receive(blocks())
+
+        receive(transfers(p))
+        vs[k + 1] = vs[k + 1] + outer(p)
+        ds[k + 1] = blockmul(prec, lambda t: vs[k + 1, t])
+        vs[k + 2] = apply(k + 1)
+        dots(k + 1, KRYLOV)
+        receive(transfers(p + 1))
+        receive(diagonals(p))
+        complete(k, p)
+        vs[k + 2] = vs[k + 2] + outer(p + 1)
         return carry
 
-    lax.fori_loop(0, KRYLOV, step, 0)
+    lax.fori_loop(0, KRYLOV // 2, two_steps, 0)
     dots(KRYLOV, KRYLOV + 1)
     slots[me] = grow[...]
 
@@ -261,7 +352,10 @@
 
     lax.fori_loop(1, count, put_all, 0)
     for p in range(KRYLOV + 1):
-        sent(p)
+        sent(transfers(p))
+    for p in range(1, KRYLOV, 2):
+        sent(diagonals(p))
+    sent(blocks())
     lax.fori_loop(1, count, take_all, 0)
     total = jnp.sum(slots[...], axis=0)
     at = lax.broadcasted_iota(jnp.int32, total.shape, 1)
@@ -299,6 +393,12 @@
             pltpu.SemaphoreType.DMA((phases, 4)), pltpu.SemaphoreType.DMA((phases, 4)),
             vmem(1, wide), vmem(rows * cols, 1, wide),
             pltpu.SemaphoreType.DMA((rows * cols,)), pltpu.SemaphoreType.DMA((rows * cols,)),
+            vmem(species, species, wide), vmem(species, species, wide), vmem(species, high, wide),
+            vmem(species, species, wide), vmem(species, species, wide),
+            vmem(species, high, wide), vmem(species, high, wide),
+            pltpu.SemaphoreType.DMA((4,)), pltpu.SemaphoreType.DMA((4,)),
+            vmem(phases, 4, 1, wide),
+            pltpu.SemaphoreType.DMA((phases, 4)), pltpu.SemaphoreType.DMA((phases, 4)),
         ],
         compiler_params=pltpu.CompilerParams(collective_id=0, has_side_effects=True),
     )(state, history, rates, quadratic, velocity.T, precond)

time: 27.8 us -> 23.8 us (0.86)
  Pallas kernels: 24.7 us -> 20.6 us
    pallas_call x1, Pallas kernels: 24.7 us -> 20.6 us  [body(): pl.pallas_call(functools.partial(kernel, rows, cols), out_shape=(pltpu.VM...]
where the time goes in v3:
time: 23.8 us; the launch traced here: 23.6 us
  Pallas kernels  20.6 us (87%)
  between operations  2.33 us (10%)
  local copies, waits for them, and re-layouts  0.64 us (3%)
    pallas_call x1, Pallas kernels, body(): pl.pallas_call(functools.partial(kernel, rows, cols), out_shape=(pltpu.VM...  20.6 us
    unnamed x1, local copies, waits for them, and re-layouts  0.64 us

profile of v3, /device:TPU:0, one launch (start us, length us, event | category | flops | bytes accessed | tf_op | source)
XLA Modules:
  0.0 23.6 jit_solution(14868649362579865130)
XLA Ops:
  0.6 20.6 %shard_map.77 = (f32[10,16,128]{2,1,0:T(8,128)S(1)}, f32[1]{0:T(128)}) custom-call(f32[10,16,128]{2,1,0:T(8,128)} %state_h.1, f32[10,16,128]{2,1,0:T(8,128)} %hist_h.1, f32[10,10,16,128]{3,2,1,0:T(8,128)} %rates_h.1, f32[10,16,128]{2,1,0:T(8,128)} %quad_h.1, f32[2,10]{1,0:T(2,128)} %bitcast.1, f32[10,10,16,128]{3,2,1,0:T(8,128)} %prec_h.1), custom_call_target="tpu_custom_call" | custom-call | tf_op jit(solution)/shard_map/pallas_call | solution.py:379
  21.3 0.6 %copy.10 = f32[10,16,128]{2,1,0:T(8,128)} copy(f32[10,16,128]{2,1,0:T(8,128)S(1)} %get-tuple-element.2) | data formatting | bytes 163840

commit v4 on v3

--- a/solution.py
+++ b/solution.py
@@ -154,16 +154,16 @@
             (right, left, make(pput_t, pgot_l, "col", my_col, 1, cols, 3)),
         ]
 
-    def transfers(p):
+    def transfers(p, lo=None, hi=None):
         def make(src, dst, axis, mine, step, size, q):
             return pltpu.make_async_remote_copy(
-                src_ref=src.at[p], dst_ref=dst.at[p], send_sem=ssem.at[p, q], recv_sem=rsem.at[p, q],
+                src_ref=src, dst_ref=dst.at[p], send_sem=ssem.at[p, q], recv_sem=rsem.at[p, q],
                 device_id={axis: lax.rem(mine + step + size, size)}, device_id_type=MESH)
         return [
-            (up, down, make(put_lo, got_hi, "row", my_row, -1, rows, 0)),
-            (down, up, make(put_hi, got_lo, "row", my_row, 1, rows, 1)),
-            (left, right, make(put_t, got_r, "col", my_col, -1, cols, 2)),
-            (right, left, make(put_t, got_l, "col", my_col, 1, cols, 3)),
+            (up, down, make(put_lo.at[p] if lo is None else lo, got_hi, "row", my_row, -1, rows, 0)),
+            (down, up, make(put_hi.at[p] if hi is None else hi, got_lo, "row", my_row, 1, rows, 1)),
+            (left, right, make(put_t.at[p], got_r, "col", my_col, -1, cols, 2)),
+            (right, left, make(put_t.at[p], got_l, "col", my_col, 1, cols, 3)),
         ]
 
     def tile_of(v):
@@ -207,28 +207,36 @@
             def _(copy=copy):
                 copy.wait_send()
 
-    def complete(k, p):
-        low, top = got_lo[p + 1], got_hi[p + 1]
-        west, east = got_l[p + 1], got_r[p + 1]
+    def own_part(k):
+        low = top = jnp.zeros((species, wide), jnp.float32)
+        west = east = jnp.zeros((high, wide), jnp.float32)
+        for t in range(species):
+            d = ds[k, t]
+            ax, ay = cx[t], cy[t]
+            low = low + pgot_lo[t] * (ax[0:1] * d[0:1])
+            top = top - pgot_hi[t] * (ax[0:1] * d[high - 1:high])
+            west = west + pgot_l[t] * (ay * d[:, 0:1])
+            east = east - pgot_r[t] * (ay * d[:, wide - 1:wide])
+        return low, top, west, east
+
+    def complete(p, own):
+        low, top, west, east = own
         first = lax.broadcasted_iota(jnp.int32, (1, wide), 1) == 0
         near_row, far_row = row_at == 0, row_at == high - 1
         lines = [got_c[p, q] for q in range(4)]
         for t in range(species):
-            d = ds[k, t]
             odd, even = (2 * t - 1) % wide, 2 * t
             ul, dl = lines[0][:, odd:odd + 1], lines[2][:, odd:odd + 1]
             ur, dr = lines[1][:, even:even + 1], lines[3][:, even:even + 1]
-            ax, ay, ends = cx[t], cy[t], cs[t, 0:1, :]
-            low = low + pgot_lo[t] * (ax[0:1] * d[0:1] + ends * jnp.where(first, ul, ur))
-            top = top + pgot_hi[t] * (ends * jnp.where(first, dl, dr) - ax[0:1] * d[high - 1:high])
-            side_l = jnp.where(near_row, -ul, jnp.where(far_row, dl, 0.0))
-            side_r = jnp.where(near_row, -ur, jnp.where(far_row, dr, 0.0))
-            west = west + pgot_l[t] * (ax * side_l + ay * d[:, 0:1])
-            east = east + pgot_r[t] * (ax * side_r - ay * d[:, wide - 1:wide])
-        got_lo[p + 1] = low
-        got_hi[p + 1] = top
-        got_l[p + 1] = west
-        got_r[p + 1] = east
+            ax, ends = cx[t], cs[t, 0:1, :]
+            low = low + pgot_lo[t] * (ends * jnp.where(first, ul, ur))
+            top = top + pgot_hi[t] * (ends * jnp.where(first, dl, dr))
+            west = west + pgot_l[t] * (ax * jnp.where(near_row, -ul, jnp.where(far_row, dl, 0.0)))
+            east = east + pgot_r[t] * (ax * jnp.where(near_row, -ur, jnp.where(far_row, dr, 0.0)))
+        got_lo[p + 1] += low
+        got_hi[p + 1] += top
+        got_l[p + 1] += west
+        got_r[p + 1] += east
 
     def inner(v):
         parts = []
@@ -267,14 +275,16 @@
             line = jnp.where(at == k * (KRYLOV + 1) + j, value, line)
         grow[...] = line
 
-    copies[0].wait()
-    pack(0, y[...])
     if near:
         beside = sum(there.astype(jnp.int32) for there in (up, down, left, right))
         pl.semaphore_wait(barrier, beside)
     else:
         pl.semaphore_wait(barrier, count - 1)
-    send(transfers(0))
+    state_out = transfers(0, state_h.at[:, 0, :], state_h.at[:, high - 1, :])
+    send(state_out[:2])
+    copies[0].wait()
+    put_t[0] = tile_of(y[...])
+    send(state_out[2:])
     copies[1].wait()
     for s in range(species):
         cx[s] = jnp.full((high, wide), 0.5 * GAMMA * vel[0, s])
@@ -292,7 +302,7 @@
     loss = quad[...] * now
     diag[...] = 1.0 + (2.0 * GAMMA) * loss
     start = hist[...] - now - GAMMA * (loss * now) + GAMMA * blockmul(rates, lambda t: y[t]) - inner(now)
-    receive(transfers(0))
+    receive(state_out)
     vs[0] = start - outer(0)
 
     def apply(k):
@@ -313,6 +323,7 @@
         def _():
             receive(blocks())
 
+        own = own_part(k)
         receive(transfers(p))
         vs[k + 1] = vs[k + 1] + outer(p)
         ds[k + 1] = blockmul(prec, lambda t: vs[k + 1, t])
@@ -320,7 +331,7 @@
         dots(k + 1, KRYLOV)
         receive(transfers(p + 1))
         receive(diagonals(p))
-        complete(k, p)
+        complete(p, own)
         vs[k + 2] = vs[k + 2] + outer(p + 1)
         return carry
 
@@ -351,7 +362,8 @@
         return carry
 
     lax.fori_loop(1, count, put_all, 0)
-    for p in range(KRYLOV + 1):
+    sent(state_out)
+    for p in range(1, KRYLOV + 1):
         sent(transfers(p))
     for p in range(1, KRYLOV, 2):
         sent(diagonals(p))

time: 23.8 us -> 23.8 us (level)
  no operation moved by 1% of the time
where the time goes in v4:
time: 23.8 us; the launch traced here: 23.6 us
  Pallas kernels  20.7 us (87%)
  between operations  2.33 us (10%)
  local copies, waits for them, and re-layouts  0.64 us (3%)
    pallas_call x1, Pallas kernels, body(): pl.pallas_call(functools.partial(kernel, rows, cols), out_shape=(pltpu.VM...  20.7 us
    unnamed x1, local copies, waits for them, and re-layouts  0.64 us

profile of v4, /device:TPU:0, one launch (start us, length us, event | category | flops | bytes accessed | tf_op | source)
XLA Modules:
  0.0 23.6 jit_solution(1335499249823985733)
XLA Ops:
  0.6 20.7 %shard_map.77 = (f32[10,16,128]{2,1,0:T(8,128)S(1)}, f32[1]{0:T(128)}) custom-call(f32[10,16,128]{2,1,0:T(8,128)} %state_h.1, f32[10,16,128]{2,1,0:T(8,128)} %hist_h.1, f32[10,10,16,128]{3,2,1,0:T(8,128)} %rates_h.1, f32[10,16,128]{2,1,0:T(8,128)} %quad_h.1, f32[2,10]{1,0:T(2,128)} %bitcast.1, f32[10,10,16,128]{3,2,1,0:T(8,128)} %prec_h.1), custom_call_target="tpu_custom_call" | custom-call | tf_op jit(solution)/shard_map/pallas_call | solution.py:391
  21.3 0.6 %copy.10 = f32[10,16,128]{2,1,0:T(8,128)} copy(f32[10,16,128]{2,1,0:T(8,128)S(1)} %get-tuple-element.2) | data formatting | bytes 163840

commit v5 on v4

--- a/solution.py
+++ b/solution.py
@@ -154,14 +154,14 @@
             (right, left, make(pput_t, pgot_l, "col", my_col, 1, cols, 3)),
         ]
 
-    def transfers(p, lo=None, hi=None):
+    def transfers(p):
         def make(src, dst, axis, mine, step, size, q):
             return pltpu.make_async_remote_copy(
                 src_ref=src, dst_ref=dst.at[p], send_sem=ssem.at[p, q], recv_sem=rsem.at[p, q],
                 device_id={axis: lax.rem(mine + step + size, size)}, device_id_type=MESH)
         return [
-            (up, down, make(put_lo.at[p] if lo is None else lo, got_hi, "row", my_row, -1, rows, 0)),
-            (down, up, make(put_hi.at[p] if hi is None else hi, got_lo, "row", my_row, 1, rows, 1)),
+            (up, down, make(put_lo.at[p], got_hi, "row", my_row, -1, rows, 0)),
+            (down, up, make(put_hi.at[p], got_lo, "row", my_row, 1, rows, 1)),
             (left, right, make(put_t.at[p], got_r, "col", my_col, -1, cols, 2)),
             (right, left, make(put_t.at[p], got_l, "col", my_col, 1, cols, 3)),
         ]
@@ -275,16 +275,15 @@
             line = jnp.where(at == k * (KRYLOV + 1) + j, value, line)
         grow[...] = line
 
+    copies[0].wait()
+    pack(0, y[...])
     if near:
         beside = sum(there.astype(jnp.int32) for there in (up, down, left, right))
         pl.semaphore_wait(barrier, beside)
     else:
         pl.semaphore_wait(barrier, count - 1)
-    state_out = transfers(0, state_h.at[:, 0, :], state_h.at[:, high - 1, :])
-    send(state_out[:2])
-    copies[0].wait()
-    put_t[0] = tile_of(y[...])
-    send(state_out[2:])
+    state_out = transfers(0)
+    send(state_out)
     copies[1].wait()
     for s in range(species):
         cx[s] = jnp.full((high, wide), 0.5 * GAMMA * vel[0, s])

time: 23.8 us -> 23.6 us (level)
  no operation moved by 1% of the time
where the time goes in v5:
time: 23.6 us; the launch traced here: 23.4 us
  Pallas kernels  20.5 us (87%)
  between operations  2.33 us (10%)
  local copies, waits for them, and re-layouts  0.64 us (3%)
    pallas_call x1, Pallas kernels, body(): pl.pallas_call(functools.partial(kernel, rows, cols), out_shape=(pltpu.VM...  20.5 us
    unnamed x1, local copies, waits for them, and re-layouts  0.64 us

profile of v5, /device:TPU:0, one launch (start us, length us, event | category | flops | bytes accessed | tf_op | source)
XLA Modules:
  0.0 23.4 jit_solution(9653628359793434905)
XLA Ops:
  0.6 20.5 %shard_map.77 = (f32[10,16,128]{2,1,0:T(8,128)S(1)}, f32[1]{0:T(128)}) custom-call(f32[10,16,128]{2,1,0:T(8,128)} %state_h.1, f32[10,16,128]{2,1,0:T(8,128)} %hist_h.1, f32[10,10,16,128]{3,2,1,0:T(8,128)} %rates_h.1, f32[10,16,128]{2,1,0:T(8,128)} %quad_h.1, f32[2,10]{1,0:T(2,128)} %bitcast.1, f32[10,10,16,128]{3,2,1,0:T(8,128)} %prec_h.1), custom_call_target="tpu_custom_call" | custom-call | tf_op jit(solution)/shard_map/pallas_call | solution.py:390
  21.1 0.6 %copy.10 = f32[10,16,128]{2,1,0:T(8,128)} copy(f32[10,16,128]{2,1,0:T(8,128)S(1)} %get-tuple-element.2) | data formatting | bytes 163840
